TPU v7x, 32 devices: a whole 2x2x4 slice. The times are simulated.
32 devices in a mesh: dp: 8 (over z, x), shard: 4 (over y, core).
Axes of the slice: x: 2, y: 2, z: 4, core: 2. Of those that a mesh axis runs over, the one named last changes fastest.
Arguments:
- noisy: float32 [128, 256, 16], P(('dp', 'shard')), may hold values from -6 to 6
- velocity: float32 [128, 256, 16], P(('dp', 'shard')), may hold values from -6 to 6
- tstep_idx: int32 [128], P(('dp', 'shard')), may hold values from 0 to 999
- class_ids: int32 [128], P(('dp', 'shard')), may hold values from 0 to 1000
- time_weight: float32 [128], P(('dp', 'shard')), may hold values from 0.3 to 3
- dino: bfloat16 [128, 256, 768], P(('dp', 'shard')), may hold values from -6 to 6
- owner_map: int32 [12], replicated, may hold values from 0 to 11, each once
- adam_flat: float32 [2129920], P(('dp', 'shard')), may hold values from -4 to 4
- adam_m: float32 [2129920], P(('dp', 'shard')), may hold values from -0.015625 to 0.015625
- adam_v: float32 [2129920], P(('dp', 'shard')), may hold values from 1e-06 to 0.0001
- blocks_w: float32 [12, 384, 384], P('shard'), may hold values from -0.3125 to 0.3125
- stat_left: float32 [12, 384, 384], P('shard'), may hold values from -0.005 to 0.01, as said below
- stat_right: float32 [12, 384, 384], P('shard'), may hold values from -0.005 to 0.01, as said below
- root_left: float32 [12, 384, 384], P('shard'), may hold values from -3 to 3, as said below
- root_right: float32 [12, 384, 384], P('shard'), may hold values from -3 to 3, as said below
Outputs:
- loss: float32 [], replicated
- block_update: float32 [12, 384, 384], P('shard')
- stat_left_new: float32 [12, 384, 384], P('shard')
- stat_right_new: float32 [12, 384, 384], P('shard')
- adam_update: float32 [2129920], P(('dp', 'shard'))
- adam_m_new: float32 [2129920], P(('dp', 'shard'))
- adam_v_new: float32 [2129920], P(('dp', 'shard'))
Inputs may be any that keep to these rules, and one draw needn't show every extreme that they name: `owner_map`: each block number appears once. `stat_left`: each slot is symmetric positive definite. `stat_right`: each slot is symmetric positive definite. `root_left`: each slot is symmetric positive definite. `root_right`: each slot is symmetric positive definite.
All inputs are finite; a program needn't handle non-finite values.
Results may differ from a plain program's by a relative error of at most 0.0097.
Values may be sent and summed in bfloat16 or wider, within the bound.
No kernel may reach another device: no remote copies, remote signals or barrier semaphores. Data moves between devices by JAX's collectives and lax.ppermute only.
A program may use at most 192 MiB of HBM per device.

v0:
```python
import functools
import math
import jax
import jax.numpy as jnp
from jax import lax
from jax.sharding import PartitionSpec as P

D = 384
HEADS = 6
HDIM = 64
F = 1536
PD = 16
GRID = 16
SEQ = 256
FREQ = 256
NCLS = 1001
DINO = 768
STEP = 10
NBLK = 12
ADAM_LEN = 2125072
ADAM_PAD = 2129920
HIGHEST = lax.Precision.HIGHEST
BETA_ONE = 0.9
BETA_TWO = 0.95
ADAM_EPS = 1e-08
ADAM_RATE = 0.01
DECAY_RATE = 0.1
STAT_BETA = 0.9
SHAMPOO_RATE = 0.02
RMS_EPS = 1e-08
REPA_WEIGHT = 0.5
NORM_EPS = 1e-06


def segment_shapes():
    return [
        (PD, D),
        (D,),
        (FREQ, D),
        (D,),
        (D, D),
        (D,),
        (NCLS, D),
        (D, 6 * D),
        (6 * D,),
        (D,),
        (D,),
        (D,),
        (F,),
        (D,),
        (D, 2 * D),
        (2 * D,),
        (D, PD),
        (PD,),
        (D, DINO),
        (DINO,),
    ]


def unflatten(flat):
    pieces = []
    offset = 0
    for seg_dims in segment_shapes():
        length = math.prod(seg_dims)
        pieces.append(flat[offset : offset + length].reshape(seg_dims))
        offset += length
    return pieces


def position_table():
    quarter = D // 4
    frequencies = 1.0 / 10000.0 ** (jnp.arange(quarter, dtype=jnp.float32) / quarter)
    cell_ids = jnp.arange(SEQ, dtype=jnp.int32)
    row_arg = (cell_ids // GRID).astype(jnp.float32)[:, None] * frequencies[None, :]
    col_arg = (cell_ids % GRID).astype(jnp.float32)[:, None] * frequencies[None, :]
    return jnp.concatenate(
        [jnp.sin(col_arg), jnp.cos(col_arg), jnp.sin(row_arg), jnp.cos(row_arg)], axis=1
    )


def time_features(tstep_idx):
    half_freq = FREQ // 2
    frequencies = jnp.exp(-math.log(10000.0) * jnp.arange(half_freq, dtype=jnp.float32) / half_freq)
    angles = (tstep_idx.astype(jnp.float32) + 0.5)[:, None] * frequencies[None, :]
    return jnp.concatenate([jnp.cos(angles), jnp.sin(angles)], axis=1)


def normalize(values):
    centered = values - jnp.mean(values, axis=-1, keepdims=True)
    inv_dev = lax.rsqrt(jnp.mean(centered * centered, axis=-1, keepdims=True) + NORM_EPS)
    return (centered * inv_dev, inv_dev)


def normalize_back(grad_in, normed, inv_dev):
    return inv_dev * (
        grad_in
        - jnp.mean(grad_in, axis=-1, keepdims=True)
        - normed * jnp.mean(grad_in * normed, axis=-1, keepdims=True)
    )


def condition_terms(
    tstep_idx,
    class_ids,
    time_in_weight,
    time_in_bias,
    time_out_weight,
    time_out_bias,
    class_table,
    mod_weight,
    mod_bias,
    final_mod_weight,
    final_mod_bias,
):
    features = time_features(tstep_idx)
    time_hidden = jax.nn.silu(jnp.dot(features, time_in_weight, precision=HIGHEST) + time_in_bias)
    onehot_class = (class_ids[:, None] == jnp.arange(NCLS, dtype=jnp.int32)[None, :]).astype(
        jnp.float32
    )
    condition = (
        jnp.dot(time_hidden, time_out_weight, precision=HIGHEST)
        + time_out_bias
        + jnp.dot(onehot_class, class_table, precision=HIGHEST)
    )
    cond_act = jax.nn.silu(condition)
    modulation = jnp.dot(cond_act, mod_weight, precision=HIGHEST) + mod_bias
    final_mods = jnp.dot(cond_act, final_mod_weight, precision=HIGHEST) + final_mod_bias
    return (modulation, final_mods)


def cosine_total(aligned, dino_f):
    products = jnp.sum(aligned * dino_f, axis=-1)
    return jnp.sum(
        products
        * lax.rsqrt(jnp.sum(aligned * aligned, axis=-1) + NORM_EPS)
        * lax.rsqrt(jnp.sum(dino_f * dino_f, axis=-1) + NORM_EPS)
    )


def matmul(left, right):
    return jnp.dot(left, right, preferred_element_type=jnp.float32)


def row_total(rounded):
    return jnp.sum(rounded.astype(jnp.float32), axis=0)


def body(
    noisy,
    velocity,
    tstep_idx,
    class_ids,
    time_weight,
    dino,
    owner_map,
    adam_flat,
    adam_m,
    adam_v,
    blocks_w,
    stat_left,
    stat_right,
    root_left,
    root_right,
):
    devices = lax.axis_size("dp") * lax.axis_size("shard")
    images = noisy.shape[0]
    seq = noisy.shape[1]
    total_img = images * devices
    rows = images * seq
    fc_ratio = F // D
    flat_low = lax.all_gather(adam_flat.astype(jnp.bfloat16), ("dp", "shard"), axis=0, tiled=True)
    slot_low = lax.all_gather(blocks_w.astype(jnp.bfloat16), "shard", axis=0, tiled=True)
    block_ids = jnp.arange(NBLK, dtype=jnp.int32)
    slot_of = jnp.sum(
        block_ids[:, None] * (owner_map[:, None] == block_ids[None, :]).astype(jnp.int32), axis=0
    )
    blocks = jnp.take(slot_low, slot_of, axis=0)
    w_qkv = jnp.concatenate([blocks[0], blocks[1], blocks[2]], axis=1)
    w_proj = blocks[3]
    w_up = jnp.concatenate([blocks[4 + which] for which in range(fc_ratio)], axis=1)
    w_down = blocks[4 + fc_ratio :].reshape(F, D)
    pieces_low = unflatten(flat_low)
    pieces = [piece.astype(jnp.float32) for piece in pieces_low]
    (
        patch_weight,
        patch_bias,
        time_in_weight,
        time_in_bias,
        time_out_weight,
        time_out_bias,
        class_table,
        mod_weight,
        mod_bias,
        query_bias,
        value_bias,
        proj_bias,
        hidden_bias,
        down_bias,
        final_mod_weight,
        final_mod_bias,
        final_weight,
        final_bias,
        align_weight,
        align_bias,
    ) = pieces
    patch_low = pieces_low[0]
    final_low = pieces_low[16]
    align_low = pieces_low[18]
    cond_weights = (
        time_in_weight,
        time_in_bias,
        time_out_weight,
        time_out_bias,
        class_table,
        mod_weight,
        mod_bias,
        final_mod_weight,
        final_mod_bias,
    )
    (modulation, final_mods), cond_back = jax.vjp(
        functools.partial(condition_terms, tstep_idx, class_ids), *cond_weights
    )
    shift_one, scale_one, gate_one, shift_two, scale_two, gate_two = [
        modulation[:, None, which * D : (which + 1) * D] for which in range(6)
    ]
    final_shift = final_mods[:, None, :D]
    final_scale = final_mods[:, None, D:]
    noisy_low = noisy.astype(jnp.bfloat16).reshape(rows, PD)
    hidden0 = (matmul(noisy_low, patch_low) + patch_bias).reshape(images, seq, D) + position_table()
    norm_one, inv_one = normalize(hidden0)
    act_one = (norm_one * (1.0 + scale_one) + shift_one).astype(jnp.bfloat16).reshape(rows, D)
    qkv_bias = jnp.concatenate([query_bias, jnp.zeros((D,), jnp.float32), value_bias])
    projected = (
        (matmul(act_one, w_qkv) + qkv_bias)
        .astype(jnp.bfloat16)
        .reshape(images, seq, 3, HEADS, HDIM)
    )
    queries = projected[:, :, 0]
    key_part = projected[:, :, 1]
    values = projected[:, :, 2]
    scale_qk = HDIM ** (-0.5)
    scores = (
        jnp.einsum("gqhe,gkhe->ghqk", queries, key_part, preferred_element_type=jnp.float32)
        * scale_qk
    )
    row_max = jnp.max(scores, axis=-1, keepdims=True)
    log_total = row_max + jnp.log(jnp.sum(jnp.exp(scores - row_max), axis=-1, keepdims=True))
    probs_low = jnp.exp(scores - log_total).astype(jnp.bfloat16)
    attended = (
        jnp.einsum("ghqk,gkhe->gqhe", probs_low, values, preferred_element_type=jnp.float32)
        .reshape(rows, D)
        .astype(jnp.bfloat16)
    )
    branch_one = (matmul(attended, w_proj) + proj_bias).reshape(images, seq, D)
    hidden1 = hidden0 + gate_one * branch_one
    norm_two, inv_two = normalize(hidden1)
    act_two = (norm_two * (1.0 + scale_two) + shift_two).astype(jnp.bfloat16).reshape(rows, D)
    inner_pre = matmul(act_two, w_up) + hidden_bias
    gelu_out, gelu_back = jax.vjp(functools.partial(jax.nn.gelu, approximate=True), inner_pre)
    gelu_low = gelu_out.astype(jnp.bfloat16)
    branch_two = (matmul(gelu_low, w_down) + down_bias).reshape(images, seq, D)
    hidden2 = hidden1 + gate_two * branch_two
    norm_three, inv_three = normalize(hidden2)
    act_three = (
        (norm_three * (1.0 + final_scale) + final_shift).astype(jnp.bfloat16).reshape(rows, D)
    )
    output = (matmul(act_three, final_low) + final_bias).reshape(images, seq, PD)
    errors = output - velocity
    main_term = jnp.sum(time_weight[:, None, None] * errors * errors) / (total_img * SEQ * PD)
    hidden1_low = hidden1.astype(jnp.bfloat16).reshape(rows, D)
    aligned = matmul(hidden1_low, align_low) + align_bias
    dino_f = dino.astype(jnp.float32).reshape(rows, DINO)
    cosine_sum, cosine_back = jax.vjp(functools.partial(cosine_total, dino_f=dino_f), aligned)
    align_scale = REPA_WEIGHT / (total_img * SEQ)
    loss_local = main_term - align_scale * cosine_sum
    back_output = (
        (2.0 * time_weight[:, None, None] * errors / (total_img * SEQ * PD))
        .reshape(rows, PD)
        .astype(jnp.bfloat16)
    )
    grad_final = matmul(act_three.T, back_output)
    grad_final_bias = row_total(back_output)
    back_three = matmul(back_output, final_low.T).reshape(images, seq, D)
    grad_final_shift = jnp.sum(back_three, axis=1)
    grad_final_scale = jnp.sum(back_three * norm_three, axis=1)
    back_hidden2 = normalize_back(back_three * (1.0 + final_scale), norm_three, inv_three)
    back_branch_two = (back_hidden2 * gate_two).reshape(rows, D).astype(jnp.bfloat16)
    grad_gate_two = jnp.sum(back_hidden2 * branch_two, axis=1)
    grad_down = matmul(gelu_low.T, back_branch_two)
    grad_down_bias = row_total(back_branch_two)
    back_inner = gelu_back(matmul(back_branch_two, w_down.T))[0].astype(jnp.bfloat16)
    grad_up = matmul(act_two.T, back_inner)
    grad_hidden_bias = row_total(back_inner)
    back_two = matmul(back_inner, w_up.T).reshape(images, seq, D)
    grad_shift_two = jnp.sum(back_two, axis=1)
    grad_scale_two = jnp.sum(back_two * norm_two, axis=1)
    back_aligned = cosine_back(jnp.asarray(-align_scale, jnp.float32))[0].astype(jnp.bfloat16)
    grad_align = matmul(hidden1_low.T, back_aligned)
    grad_align_bias = row_total(back_aligned)
    back_hidden1 = (
        back_hidden2
        + normalize_back(back_two * (1.0 + scale_two), norm_two, inv_two)
        + matmul(back_aligned, align_low.T).reshape(images, seq, D)
    )
    back_branch_one = (back_hidden1 * gate_one).reshape(rows, D).astype(jnp.bfloat16)
    grad_gate_one = jnp.sum(back_hidden1 * branch_one, axis=1)
    grad_proj = matmul(attended.T, back_branch_one)
    grad_proj_bias = row_total(back_branch_one)
    back_attended = (
        matmul(back_branch_one, w_proj.T).astype(jnp.bfloat16).reshape(images, seq, HEADS, HDIM)
    )
    back_probs = jnp.einsum(
        "gqhe,gkhe->ghqk", back_attended, values, preferred_element_type=jnp.float32
    )
    grad_values = jnp.einsum(
        "ghqk,gqhe->gkhe", probs_low, back_attended, preferred_element_type=jnp.float32
    )
    scores_again = (
        jnp.einsum("gqhe,gkhe->ghqk", queries, key_part, preferred_element_type=jnp.float32)
        * scale_qk
    )
    probs_again = jnp.exp(scores_again - log_total)
    back_scores = (
        probs_again * (back_probs - jnp.sum(back_probs * probs_again, axis=-1, keepdims=True))
    ).astype(jnp.bfloat16)
    grad_queries = (
        jnp.einsum("ghqk,gkhe->gqhe", back_scores, key_part, preferred_element_type=jnp.float32)
        * scale_qk
    )
    grad_keys = (
        jnp.einsum("ghqk,gqhe->gkhe", back_scores, queries, preferred_element_type=jnp.float32)
        * scale_qk
    )
    back_projected = (
        jnp.stack([grad_queries, grad_keys, grad_values], axis=2)
        .reshape(rows, 3 * D)
        .astype(jnp.bfloat16)
    )
    grad_qkv = matmul(act_one.T, back_projected)
    grad_qkv_bias = row_total(back_projected)
    back_one = matmul(back_projected, w_qkv.T).reshape(images, seq, D)
    grad_shift_one = jnp.sum(back_one, axis=1)
    grad_scale_one = jnp.sum(back_one * norm_one, axis=1)
    back_hidden0 = (
        (back_hidden1 + normalize_back(back_one * (1.0 + scale_one), norm_one, inv_one))
        .reshape(rows, D)
        .astype(jnp.bfloat16)
    )
    grad_patch = matmul(noisy_low.T, back_hidden0)
    grad_patch_bias = row_total(back_hidden0)
    grad_modulation = jnp.concatenate(
        [
            grad_shift_one,
            grad_scale_one,
            grad_gate_one,
            grad_shift_two,
            grad_scale_two,
            grad_gate_two,
        ],
        axis=1,
    )
    grad_final_mods = jnp.concatenate([grad_final_shift, grad_final_scale], axis=1)
    cond_grads = cond_back((grad_modulation, grad_final_mods))
    grad_list = (
        [grad_patch, grad_patch_bias]
        + list(cond_grads[:7])
        + [
            grad_qkv_bias[:D],
            grad_qkv_bias[2 * D :],
            grad_proj_bias,
            grad_hidden_bias,
            grad_down_bias,
            cond_grads[7],
            cond_grads[8],
            grad_final,
            grad_final_bias,
            grad_align,
            grad_align_bias,
        ]
    )
    flat_grad = jnp.concatenate(
        [gradient_part.reshape(-1) for gradient_part in grad_list]
        + [jnp.zeros((ADAM_PAD - ADAM_LEN,), jnp.float32)]
    )
    grad_model = jnp.concatenate(
        [
            grad_qkv.reshape(D, 3, D).transpose(1, 0, 2),
            grad_proj[None],
            grad_up.reshape(D, fc_ratio, D).transpose(1, 0, 2),
            grad_down.reshape(fc_ratio, D, D),
        ],
        axis=0,
    )
    grad_slot = jnp.take(grad_model, owner_map, axis=0)
    flat_owned = lax.psum_scatter(flat_grad, ("dp", "shard"), scatter_dimension=0, tiled=True)
    loss_total = lax.psum(loss_local, ("dp", "shard"))
    summed = lax.psum(grad_slot, "dp")
    owned = lax.psum_scatter(
        summed.astype(jnp.bfloat16), "shard", scatter_dimension=0, tiled=True
    ).astype(jnp.float32)
    new_left = STAT_BETA * stat_left + (1.0 - STAT_BETA) * jnp.einsum(
        "bij,bkj->bik", owned, owned, precision=HIGHEST
    )
    new_right = STAT_BETA * stat_right + (1.0 - STAT_BETA) * jnp.einsum(
        "bji,bjk->bik", owned, owned, precision=HIGHEST
    )
    left_applied = jnp.einsum("bij,bjk->bik", root_left, owned, precision=HIGHEST)
    direction = jnp.einsum("bij,bjk->bik", left_applied, root_right, precision=HIGHEST)
    root_mean = jnp.sqrt(jnp.mean(direction * direction, axis=(1, 2), keepdims=True))
    block_update = -SHAMPOO_RATE * (direction / (root_mean + RMS_EPS) + DECAY_RATE * blocks_w)
    new_m = BETA_ONE * adam_m + (1.0 - BETA_ONE) * flat_owned
    new_v = BETA_TWO * adam_v + (1.0 - BETA_TWO) * flat_owned * flat_owned
    corrected_m = new_m / (1.0 - BETA_ONE**STEP)
    corrected_v = new_v / (1.0 - BETA_TWO**STEP)
    adam_update = -ADAM_RATE * (
        corrected_m / (jnp.sqrt(corrected_v) + ADAM_EPS) + DECAY_RATE * adam_flat
    )
    return (loss_total, block_update, new_left, new_right, adam_update, new_m, new_v)


def solution(mesh):
    return jax.shard_map(
        body,
        mesh=mesh,
        in_specs=(
            P(("dp", "shard"), None, None),
            P(("dp", "shard"), None, None),
            P(("dp", "shard")),
            P(("dp", "shard")),
            P(("dp", "shard")),
            P(("dp", "shard"), None, None),
            P(),
            P(("dp", "shard")),
            P(("dp", "shard")),
            P(("dp", "shard")),
            P("shard", None, None),
            P("shard", None, None),
            P("shard", None, None),
            P("shard", None, None),
            P("shard", None, None),
        ),
        out_specs=(
            P(),
            P("shard", None, None),
            P("shard", None, None),
            P("shard", None, None),
            P(("dp", "shard")),
            P(("dp", "shard")),
            P(("dp", "shard")),
        ),
        check_vma=False,
    )
```

profile of v0, /device:TPU:0, one launch (start us, length us, event | category | flops | bytes accessed | tf_op | source)
XLA Modules:
  0.0 797.5 jit_solution(3456417252762726016)
XLA Ops:
  7.3 2.6 convert_element_type.209
  17.3 26.3 %all-gather.5.cloned.1.call-done = bf16[12,384,384]{2,1,0:T(8,128)(2,1)} async-done(((bf16[3,384,384]{2,1,0:T(8,128)(2,1)}), bf16[12,384,384]{2,1,0:T(8,128)(2,1)}) %all-gather.5.cloned.1.call-update) | async-done | bytes 3538960 | tf_op jit(solution)/shard_map/all_gather | solution.py:172
  43.6 5.1 gather_fusion
  48.7 2.5 broadcast_select_fusion.1
  54.7 54.4 %all-gather.3.cloned.1.call-done = bf16[2129920]{0:T(1024)(128)(2,1)} async-done(((bf16[66560]{0:T(1024)(128)(2,1)}), bf16[2129920]{0:T(1024)(128)(2,1)}) %all-gather.3.cloned.1.call-update) | async-done | bytes 4259856 | tf_op jit(solution)/shard_map/all_gather | solution.py:171
  109.1 1.7 fusion.108
  121.1 1.9 slice.198
  122.9 3.3 reshape.435
  137.7 2.9 fusion.19
  140.5 4.3 copy.90
  144.9 6.1 reshape.436
  151.0 2.4 fusion.110
  159.4 3.6 fusion.106
  162.9 1.8 multiply_reduce_fusion.12
  165.3 1.9 fusion.26
  168.0 1.8 convolution_add_fusion.1
  169.8 3.8 fusion.104
  174.2 1.8 multiply_reduce_fusion.11
  178.0 1.9 fusion.27
  182.8 2.9 multiply_reduce_fusion.7
  185.8 2.2 convert_reduce_fusion.3
  188.0 7.3 fusion.13
  195.3 5.1 convert_reduce_fusion
  200.5 3.1 fusion.33
  203.7 3.5 multiply_reduce_fusion.2
  210.2 3.0 convert_reduce_fusion.4
  214.0 2.5 convolution_convert_fusion.1
  216.6 2.3 copy.98
  218.8 2.8 reshape.446
  221.7 7.7 multiply_reduce_fusion
  229.4 6.3 multiply_convert_fusion
  237.3 2.0 multiply_bitcast_fusion
  239.2 2.2 convolution_bitcast_fusion.2
  241.5 2.2 multiply_reduce_fusion.4
  247.1 2.5 multiply_reduce_fusion.6
  249.7 2.7 convert_reduce_fusion.5
  252.4 4.8 fusion.95
  257.8 2.1 fusion.113
  259.9 2.3 fusion.55
  262.2 1.7 fusion.91
  265.5 3.4 fusion.46
  268.9 2.2 fusion.68
  271.7 3.4 copy.104
  276.5 4.7 reshape.451
  283.6 2.1 fusion.72
  285.7 1.8 reshape.448
  287.5 2.0 convolution_bitcast_fusion.4
  291.9 2.4 reshape.452
  300.5 87.2 %concatenate.35 = f32[2129920]{0:T(1024)} concatenate(f32[6144]{0:T(1024)} %reshape.447, f32[384]{0:T(512)} %get-tuple-element.39, f32[98304]{0:T(1024)S(1)} %copy-done.57, f32[384]{0:T(512)} %get-tuple-element.37, f32[147456]{0:T(1024)S(1)} %reshape.449, f32[384]{0:T(512)} %get-tuple-element.110, f32[384384]{0:T(1024)} %reshape.450, f32[884736]{0:T(1024)} %reshape.451, ...), dimensions={0} | concatenate | bytes 17039360 | tf_op jit(solution)/shard_map/concatenate | solution.py:381
  387.8 2.3 copy.141
  391.3 4.9 copy.131
  396.2 5.1 convolution_bitcast_fusion
  401.3 4.7 copy.132
  406.1 4.2 fusion.114
  410.3 3.3 pad_maximum_fusion
  413.5 7.0 gather_fusion.1
  420.6 6.6 broadcast_select_fusion
  427.1 306.0 %all-reduce.5 = bf16[12,384,384]{2,1,0:T(8,128)(2,1)} all-reduce(f32[12,384,384]{2,1,0:T(8,128)} %broadcast_select_fusion), channel_id=1, replica_groups=mesh['dp'=8,'shard'=4] {'dp'}, use_global_device_ids=true, to_apply=%region_20.21 | all-reduce | flops 1769472 | bytes 10616832 | tf_op jit(solution)/shard_map/psum | solution.py:397
  734.7 40.7 %psum.14 = f32[]{:T(128)} all-reduce(f32[]{:T(128)S(6)} %sub.143), channel_id=1, replica_groups=mesh['dp'=8,'shard'=4] {'dp','shard'}, use_global_device_ids=true, to_apply=%region_14.15 | all-reduce | flops 1 | bytes 8 | tf_op jit(solution)/shard_map/psum | solution.py:396
  775.4 2.2 add_multiply_fusion.1
  777.5 3.0 fusion.115
  780.6 3.8 multiply_reduce_fusion.3
  786.8 2.0 multiply_add_fusion
  788.8 2.0 multiply_add_fusion.1
  (328 shorter events, 73.1 us)
Async XLA Ops:
  7.2 773.4 %copy-start = (f32[3,384,384]{2,1,0:T(8,128)S(1)}, f32[3,384,384]{2,1,0:T(8,128)}, u32[]{:S(2)}) copy-start(f32[3,384,384]{2,1,0:T(8,128)} %param.29) | copy-start | bytes 5308420
  7.2 4.5 copy-start.78
  7.2 5.1 copy-start.22
  7.2 36.4 %all-gather.5.cloned.1.call-start = ((), (), s32[]{:S(2)}) async-start(), calls=%async_computation.2 | async-start | bytes 4423680 | tf_op jit(solution)/shard_map/all_gather | solution.py:172
  9.9 3.5 copy-start.97
  9.9 99.2 %all-gather.3.cloned.1.call-start = ((), (), s32[]{:S(2)}) async-start(), calls=%async_computation.1 | async-start | bytes 4392960 | tf_op jit(solution)/shard_map/all_gather | solution.py:171
  11.6 5.1 copy-start.98
  11.6 5.1 copy-start.96
  11.6 763.7 %all-reduce.4.cloned.1.call-start = ((), (), s32[]{:S(2)}) async-start(), calls=%async_computation.4 | async-start | bytes 17039360
  17.3 114.4 %copy-start.88 = (f32[4,128]{1,0:T(4,128)}, f32[4,128]{1,0:T(4,128)S(1)}, u32[]{:S(2)}) copy-start(f32[4,128]{1,0:T(4,128)S(1)} %get-tuple-element.90) | copy-start | bytes 6148
  17.3 114.4 %copy-start.90 = (f32[4,128]{1,0:T(4,128)}, f32[4,128]{1,0:T(4,128)S(1)}, u32[]{:S(2)}) copy-start(f32[4,128]{1,0:T(4,128)S(1)} %get-tuple-element.91) | copy-start | bytes 6148
  128.4 3.3 copy-start.67
  128.4 3.5 copy-start.49
  128.4 3.8 copy-start.48
  128.4 3.8 copy-start.93
  130.0 3.8 copy-start.41
  130.1 4.8 copy-start.17
  131.7 4.6 copy-start.86
  131.9 4.4 copy-start.8
  136.3 4.3 copy-start.80
  159.1 3.8 copy-start.30
  169.8 3.8 copy-start.13
  169.8 6.8 copy-start.82
  178.0 3.2 copy-start.79
  178.0 4.8 copy-start.5
  178.0 4.8 copy-start.10
  178.0 4.8 copy-start.84
  178.0 4.8 copy-start.91
  180.8 7.1 slice-start.2
  182.8 2.9 copy-start.71
  182.8 5.2 slice-start.3
  188.0 7.3 copy-start.66
  195.3 5.1 copy-start.3
  195.3 5.1 copy-start.59
  195.3 5.1 copy-start.61
  195.3 5.1 copy-start.63
  195.3 5.1 copy-start.65
  200.5 3.2 copy-start.85
  203.7 3.5 copy-start.6
  203.7 3.5 copy-start.11
  203.7 3.5 copy-start.24
  203.7 3.5 copy-start.83
  210.0 3.1 copy-start.20
  221.7 17.5 %slice-start = ((s8[6291456]{0:T(1024)(128)(4,1)}), s8[4194304]{0:T(1024)(128)(4,1)S(1)}, s32[]{:S(2)}) async-start(s8[6291456]{0:T(1024)(128)(4,1)} %bitcast.283), calls=%async_computation.5 | async-start | bytes 8388608
  229.4 6.4 copy-start.26
  229.4 9.8 %slice-start.1 = ((s8[6291456]{0:T(1024)(128)(4,1)}), s8[2097152]{0:T(1024)(128)(4,1)S(1)}, s32[]{:S(2)}) async-start(s8[6291456]{0:T(1024)(128)(4,1)} %bitcast.283), calls=%async_computation.6 | async-start | bytes 4194304
  252.4 4.8 copy-start.42
  252.4 5.3 copy-start.18
  257.2 2.7 copy-start.94
  257.7 6.1 copy-start.50
  257.7 7.7 copy-start.4
  265.5 6.2 copy-start.16
  271.6 3.4 copy-start.28
  271.6 3.4 copy-start.31
  276.5 4.7 copy-start.40
  282.4 8.4 %copy-start.38 = (f32[384,768]{1,0:T(8,128)S(1)}, f32[384,768]{1,0:T(8,128)}, u32[]{:S(2)}) copy-start(f32[384,768]{1,0:T(8,128)} %fusion.46) | copy-start | bytes 3538948
  291.9 6.4 copy-start.33
  291.9 8.6 %copy-start.57 = (f32[98304]{0:T(1024)S(1)}, f32[98304]{0:T(1024)}, u32[]{:S(2)}) copy-start(f32[98304]{0:T(1024)} %reshape.448) | copy-start | bytes 1179652
  387.7 389.8 %reduce-scatter.2.cloned.1.call-start = ((), (), s32[]{:S(2)}) async-start(), calls=%async_computation.3 | async-start | bytes 4423680 | tf_op jit(solution)/shard_map/reduce_scatter | solution.py:398
  406.1 4.2 copy-start.52
  406.1 4.2 copy-start.53
  413.5 7.0 copy-start.95
  733.2 44.4 %copy-start.54 = (f32[3,384,384]{2,1,0:T(8,128)S(1)}, f32[3,384,384]{2,1,0:T(8,128)}, u32[]{:S(2)}) copy-start(f32[3,384,384]{2,1,0:T(8,128)} %param.28) | copy-start | bytes 5308420
  780.6 3.8 copy-start.29
  (43 other events, 81.9 us)
Sparse Core Ops, SparseCore 0:
  10.1 33.4 all-gather.4
  47.1 61.9 all-gather.2
  387.8 243.0 all-reduce.3
  733.3 39.5 reduce-scatter.1
where the time goes:
time: 810 us; the launch traced here: 798 us
  blocking collectives  347 us (43%)
  local copies, waits for them, and re-layouts  186 us (23%)
  matrix products  103 us (13%)
  waiting for transfers between devices  80.8 us (10%)
  other arithmetic  64.9 us (8%)
  between operations  16.6 us (2%)
    psum x1, blocking collectives, body(): summed = lax.psum(grad_slot, 'dp')  306 us
    concatenate x1, local copies, waits for them, and re-layouts, body(): jnp.concatenate([gradient_part.reshape(-1) for gradient_part in grad_list...  87.2 us
    dot_general x20, matrix products, matmul(): return jnp.dot(left, right, preferred_element_type=jnp.float32)  57.1 us
    all_gather x1, waiting for transfers between devices, body(): lax.all_gather(adam_flat.astype(jnp.bfloat16), ('dp', 'shard'), axis=0, t...  54.4 us
    psum x1, blocking collectives, body(): loss_total = lax.psum(loss_local, ('dp', 'shard'))  40.7 us
    all_gather x1, waiting for transfers between devices, body(): lax.all_gather(blocks_w.astype(jnp.bfloat16), 'shard', axis=0, tiled=True)  26.3 us
  transfers between devices with their start and end apart: 4, of which 2 were waited for; matrix products, arithmetic and copies ran while one was open for 7% of the time, Pallas kernels for 0%

commit v1 on v0

--- a/solution.py
+++ b/solution.py
@@ -394,7 +394,7 @@
     grad_slot = jnp.take(grad_model, owner_map, axis=0)
     flat_owned = lax.psum_scatter(flat_grad, ("dp", "shard"), scatter_dimension=0, tiled=True)
     loss_total = lax.psum(loss_local, ("dp", "shard"))
-    summed = lax.psum(grad_slot, "dp")
+    summed = jnp.sum(lax.all_gather(grad_slot, "dp"), axis=0)
     owned = lax.psum_scatter(
         summed.astype(jnp.bfloat16), "shard", scatter_dimension=0, tiled=True
     ).astype(jnp.float32)

time: 810 us -> 1610 us (1.99)
  waiting for transfers between devices: 80.8 us -> 1170 us
  blocking collectives: 347 us -> 40.9 us
  other arithmetic: 64.9 us -> 84.3 us
    all_gather x0 -> x1, waiting for transfers between devices: none -> 923 us  [body(): summed = jnp.sum(lax.all_gather(grad_slot, 'dp'), axis=0)]
    psum x1 -> x0, blocking collectives: 306 us -> none  [body(): summed = lax.psum(grad_slot, 'dp')]
    unnamed x5 -> x6, waiting for transfers between devices: 0.07 us -> 123 us
    reduce_scatter x1, waiting for transfers between devices: 0.01 us -> 40.7 us  [body(): lax.psum_scatter(summed.astype(jnp.bfloat16), 'shard', scatter_dimension=...]
    reduce_sum x0 -> x1, other arithmetic: none -> 22.2 us  [body(): summed = jnp.sum(lax.all_gather(grad_slot, 'dp'), axis=0)]
  transfers between devices with their start and end apart: 4 -> 5, of which waited for: 2 -> 5; matrix products, arithmetic and copies ran while one was open for 7% -> 12% of each run, Pallas kernels for 0% -> 0%
where the time goes in v1:
time: 1610 us; the launch traced here: 1600 us
  waiting for transfers between devices  1170 us (73%)
  local copies, waits for them, and re-layouts  189 us (12%)
  matrix products  103 us (6%)
  other arithmetic  84.3 us (5%)
  blocking collectives  40.9 us (3%)
  between operations  16.8 us (1%)
    all_gather x1, waiting for transfers between devices, body(): summed = jnp.sum(lax.all_gather(grad_slot, 'dp'), axis=0)  923 us
    unnamed x6, waiting for transfers between devices  123 us
    concatenate x1, local copies, waits for them, and re-layouts, body(): jnp.concatenate([gradient_part.reshape(-1) for gradient_part in grad_list...  87.1 us
    dot_general x20, matrix products, matmul(): return jnp.dot(left, right, preferred_element_type=jnp.float32)  60 us
    all_gather x1, waiting for transfers between devices, body(): lax.all_gather(adam_flat.astype(jnp.bfloat16), ('dp', 'shard'), axis=0, t...  54.3 us
    psum x1, blocking collectives, body(): loss_total = lax.psum(loss_local, ('dp', 'shard'))  40.9 us
    reduce_scatter x1, waiting for transfers between devices, body(): lax.psum_scatter(summed.astype(jnp.bfloat16), 'shard', scatter_dimension=...  40.7 us
  transfers between devices with their start and end apart: 5, of which 5 were waited for; matrix products, arithmetic and copies ran while one was open for 12% of the time, Pallas kernels for 0%

profile of v1, /device:TPU:0, one launch (start us, length us, event | category | flops | bytes accessed | tf_op | source)
XLA Modules:
  0.0 1601.4 jit_solution(17345270123690071206)
XLA Ops:
  7.3 2.6 convert_element_type.209
  17.2 26.4 %all-gather.6.cloned.1.call-done = bf16[12,384,384]{2,1,0:T(8,128)(2,1)} async-done(((bf16[3,384,384]{2,1,0:T(8,128)(2,1)}), bf16[12,384,384]{2,1,0:T(8,128)(2,1)}) %all-gather.6.cloned.1.call-update) | async-done | bytes 3538960 | tf_op jit(solution)/shard_map/all_gather | solution.py:172
  43.6 5.1 gather_fusion
  48.7 2.5 broadcast_select_fusion
  54.8 54.3 %all-gather.4.cloned.1.call-done = bf16[2129920]{0:T(1024)(128)(2,1)} async-done(((bf16[66560]{0:T(1024)(128)(2,1)}), bf16[2129920]{0:T(1024)(128)(2,1)}) %all-gather.4.cloned.1.call-update) | async-done | bytes 4259856 | tf_op jit(solution)/shard_map/all_gather | solution.py:171
  121.0 1.9 slice.198
  122.9 3.3 reshape.442
  137.7 2.9 fusion.19
  140.5 4.3 copy.94
  144.8 6.1 reshape.443
  150.9 2.4 fusion.110
  159.3 3.6 fusion.106
  162.9 1.8 multiply_reduce_fusion.12
  164.7 1.9 fusion.26
  167.4 1.8 convolution_add_fusion.1
  169.2 3.7 fusion.104
  173.5 1.8 multiply_reduce_fusion.11
  175.5 1.9 fusion.27
  180.3 3.5 multiply_reduce_fusion.7
  183.8 2.3 convert_reduce_fusion.3
  186.0 7.4 fusion.13
  193.4 5.1 convert_reduce_fusion
  198.6 3.1 fusion.33
  201.7 3.4 multiply_reduce_fusion.2
  209.0 3.0 convert_reduce_fusion.4
  212.9 2.5 convolution_convert_fusion.1
  215.4 2.3 copy.102
  217.7 2.8 reshape.453
  220.5 7.6 multiply_reduce_fusion
  228.1 6.5 multiply_convert_fusion
  240.7 2.0 copy.108
  243.9 2.4 convolution_bitcast_fusion.1
  246.3 5.1 copy.135
  251.4 5.0 convolution_bitcast_fusion
  256.4 4.7 copy.136
  261.0 4.0 fusion.114
  265.1 3.1 pad_maximum_fusion
  268.2 7.0 gather_fusion.1
  275.1 6.5 bitcast_select_fusion
  281.8 3.5 copy.116
  285.3 4.8 multiply_reduce_fusion.6
  290.2 2.5 convert_reduce_fusion.5
  295.7 4.8 fusion.95
  300.5 4.7 reshape.458
  306.9 2.9 fusion.113
  312.8 1.7 fusion.91
  314.5 2.1 reshape.456
  316.6 1.9 fusion.102
  319.9 1.8 reshape.455
  323.7 3.2 fusion.46
  326.9 2.3 reshape.461
  329.3 2.2 fusion.68
  331.4 2.4 reshape.459
  340.7 87.1 %concatenate.35 = f32[2129920]{0:T(1024)} concatenate(f32[6144]{0:T(1024)} %reshape.454, f32[384]{0:T(512)} %get-tuple-element.39, f32[98304]{0:T(1024)S(1)} %copy-done.54, f32[384]{0:T(512)} %get-tuple-element.37, f32[147456]{0:T(1024)S(1)} %copy-done.47, f32[384]{0:T(512)} %get-tuple-element.110, f32[384384]{0:T(1024)} %reshape.457, f32[884736]{0:T(1024)} %reshape.458, ...), dimensions={0} | concatenate | bytes 17039360 | tf_op jit(solution)/shard_map/concatenate | solution.py:381
  427.9 922.9 %all-gather.8.cloned.1.call-done = f32[8,12,384,384]{3,2,1,0:T(8,128)} async-done(((f32[1,12,384,384]{3,2,1,0:T(8,128)}), f32[8,12,384,384]{3,2,1,0:T(8,128)}) %all-gather.8.cloned.1.call-update) | async-done | bytes 56623120 | tf_op jit(solution)/shard_map/all_gather | solution.py:397
  1350.8 22.2 %reduce_sum.406 = bf16[12,384,384]{2,1,0:T(8,128)(2,1)} reduce(f32[8,12,384,384]{3,2,1,0:T(8,128)} %all-gather.8.cloned.1.call-done, f32[]{:T(128)} %constant.126.clone.1), dimensions={0}, to_apply=%region_20.21 | reduce | flops 12386304 | bytes 60162052 | tf_op jit(solution)/shard_map/reduce_sum | solution.py:397
  1374.5 40.9 %psum.7 = f32[]{:T(128)} all-reduce(f32[]{:T(128)S(6)} %sub.143), channel_id=1, replica_groups=mesh['dp'=8,'shard'=4] {'dp','shard'}, use_global_device_ids=true, to_apply=%region_14.15 | all-reduce | flops 1 | bytes 8 | tf_op jit(solution)/shard_map/psum | solution.py:396
  1415.3 123.2 %all-reduce.3.cloned.1.call-done = f32[2129920]{0:T(1024)} async-done(((f32[2129920]{0:T(1024)}), f32[2129920]{0:T(1024)}) %all-reduce.3.cloned.1.call-update) | async-done | bytes 8519696
  1538.5 2.2 add_multiply_fusion.1
  1540.7 40.7 %reduce-scatter.2.cloned.1.call-done = bf16[3,384,384]{2,1,0:T(8,128)(2,1)} async-done(((bf16[12,384,384]{2,1,0:T(8,128)(2,1)}), bf16[3,384,384]{2,1,0:T(8,128)(2,1)}) %reduce-scatter.2.cloned.1.call-update) | async-done | bytes 884752 | tf_op jit(solution)/shard_map/reduce_scatter | solution.py:398
  1581.4 3.0 fusion.115
  1584.4 3.8 multiply_reduce_fusion.3
  1590.6 2.0 multiply_add_fusion
  1592.7 2.0 multiply_add_fusion.1
  (341 shorter events, 76.7 us)
Async XLA Ops:
  7.2 1577.2 %copy-start = (f32[3,384,384]{2,1,0:T(8,128)S(1)}, f32[3,384,384]{2,1,0:T(8,128)}, u32[]{:S(2)}) copy-start(f32[3,384,384]{2,1,0:T(8,128)} %param.29) | copy-start | bytes 5308420
  7.2 4.5 copy-start.73
  7.2 5.1 copy-start.23
  7.2 36.4 %all-gather.6.cloned.1.call-start = ((), (), s32[]{:S(2)}) async-start(), calls=%async_computation.2 | async-start | bytes 4423680 | tf_op jit(solution)/shard_map/all_gather | solution.py:172
  9.9 99.2 %all-gather.4.cloned.1.call-start = ((), (), s32[]{:S(2)}) async-start(), calls=%async_computation.1 | async-start | bytes 4392960 | tf_op jit(solution)/shard_map/all_gather | solution.py:171
  11.6 5.0 copy-start.103
  11.6 5.0 copy-start.101
  11.6 1339.2 %all-gather.8.cloned.1.call-start = ((), (), s32[]{:S(2)}) async-start(), calls=%async_computation.3 | async-start | bytes 63700992 | tf_op jit(solution)/shard_map/all_gather | solution.py:397
  17.2 114.4 %copy-start.92 = (f32[4,128]{1,0:T(4,128)}, f32[4,128]{1,0:T(4,128)S(1)}, u32[]{:S(2)}) copy-start(f32[4,128]{1,0:T(4,128)S(1)} %get-tuple-element.90) | copy-start | bytes 6148
  17.2 114.4 %copy-start.94 = (f32[4,128]{1,0:T(4,128)}, f32[4,128]{1,0:T(4,128)S(1)}, u32[]{:S(2)}) copy-start(f32[4,128]{1,0:T(4,128)S(1)} %get-tuple-element.91) | copy-start | bytes 6148
  128.4 3.5 copy-start.45
  128.4 3.8 copy-start.44
  128.4 3.8 copy-start.98
  130.0 3.7 copy-start.41
  130.0 4.8 copy-start.16
  131.6 4.6 copy-start.90
  131.9 3.8 copy-start.79
  131.9 4.4 copy-start.8
  136.3 4.3 copy-start.84
  136.3 28.5 %copy-start.81 = (f32[4,384]{1,0:T(4,128)}, f32[4,384]{1,0:T(4,128)S(1)}, u32[]{:S(2)}) copy-start(f32[4,384]{1,0:T(4,128)S(1)} %get-tuple-element.117) | copy-start | bytes 18436
  159.1 3.8 copy-start.34
  164.7 42.5 %copy-start.87 = (f32[4,256]{1,0:T(4,128)}, f32[4,256]{1,0:T(4,128)S(1)}, u32[]{:S(2)}) copy-start(f32[4,256]{1,0:T(4,128)S(1)} %rsqrt.60) | copy-start | bytes 12292
  169.2 3.7 copy-start.13
  169.2 6.1 copy-start.86
  175.4 4.8 copy-start.96
  175.5 4.8 copy-start.5
  175.5 4.8 copy-start.10
  178.3 7.7 slice-start.2
  180.2 5.8 slice-start.3
  186.0 7.4 copy-start.63
  193.4 5.2 copy-start.3
  193.4 5.2 copy-start.56
  193.4 5.2 copy-start.58
  193.4 5.1 copy-start.60
  193.4 5.1 copy-start.62
  193.4 5.1 copy-start.82
  201.7 4.1 copy-start.24
  207.2 4.8 copy-start.22
  220.5 16.4 %slice-start = ((s8[6291456]{0:T(1024)(128)(4,1)}), s8[4194304]{0:T(1024)(128)(4,1)S(1)}, s32[]{:S(2)}) async-start(s8[6291456]{0:T(1024)(128)(4,1)} %bitcast.285), calls=%async_computation.6 | async-start | bytes 8388608
  228.1 6.5 copy-start.28
  228.1 8.8 slice-start.1
  261.0 4.0 copy-start.48
  261.0 4.0 copy-start.49
  261.0 4.1 copy-start.51
  268.2 7.0 copy-start.100
  281.7 3.6 copy-start.91
  281.7 3.6 copy-start.85
  281.7 1256.8 %all-reduce.3.cloned.1.call-start = ((), (), s32[]{:S(2)}) async-start(), calls=%async_computation.5 | async-start | bytes 17039360
  285.3 4.9 copy-start.7
  285.3 4.9 copy-start.12
  285.3 4.9 copy-start.40
  300.5 6.4 copy-start.17
  305.2 5.2 copy-start.99
  312.8 5.8 copy-start.93
  312.8 5.8 copy-start.95
  312.8 8.9 copy-start.74
  314.5 9.1 copy-start.4
  329.3 9.3 copy-start.33
  331.4 9.3 copy-start.76
  331.4 9.3 copy-start.47
  331.4 9.3 copy-start.54
  427.8 1153.5 %reduce-scatter.2.cloned.1.call-start = ((), (), s32[]{:S(2)}) async-start(), calls=%async_computation.4 | async-start | bytes 4423680 | tf_op jit(solution)/shard_map/reduce_scatter | solution.py:398
  1373.0 208.4 %copy-start.50 = (f32[3,384,384]{2,1,0:T(8,128)S(1)}, f32[3,384,384]{2,1,0:T(8,128)}, u32[]{:S(2)}) copy-start(f32[3,384,384]{2,1,0:T(8,128)} %param.28) | copy-start | bytes 5308420
  1584.4 3.8 copy-start.31
  (49 other events, 97.7 us)
Sparse Core Ops, SparseCore 0:
  10.1 33.4 all-gather.5
  47.1 61.9 all-gather.3
  281.8 1068.9 all-gather.7
  1356.5 181.9 all-reduce.2
  1540.9 40.4 reduce-scatter.1
